TPU v7x, 32 devices: a whole 2x2x4 slice. The times are simulated.
32 devices in a mesh: groups: 1, kcol: 16 (over z, y, x), qrow: 2 (over core).
Axes of the slice: x: 2, y: 2, z: 4, core: 2. Of those that a mesh axis runs over, the one named last changes fastest.
Arguments:
- queries: bfloat16 [128, 1024], P(('groups', 'kcol', 'qrow')), may hold values from -120 to 120
- key_value: bfloat16 [24576, 256], P(('groups', 'kcol')), may hold values from -6 to 6
- block_lists: int32 [1, 64], P('groups'), may hold values from 0 to 191, as said below
Outputs:
- attended: bfloat16 [128, 1024], P(('groups', 'kcol', 'qrow'))
Inputs may be any that keep to these rules, and one draw needn't show every extreme that they name: `block_lists`: row i names 64 distinct key blocks, none after block 191 + i (the block that holds query block i); it always names that block, the 11 blocks just before it, and block 0.
All inputs are finite; a program needn't handle non-finite values.
Results may differ from a plain program's by a relative error of at most 0.0065.
Values may be sent and summed in bfloat16 or wider, within the bound.
No kernel may reach another device: no remote copies, remote signals or barrier semaphores. Data moves between devices by JAX's collectives and lax.ppermute only.
A program may use at most 128 MiB of HBM per device.

v0:
```python
import math
import jax
import jax.numpy as jnp
from jax import lax
from jax.sharding import PartitionSpec as P

BLK = 128
masked_score = -1e30


def combined_all(part, axis, combine):
    gathered = jax.tree.map(lambda a: lax.all_gather(a, axis), part)

    def take(source):
        return jax.tree.map(lambda a: lax.dynamic_index_in_dim(a, source, 0, False), gathered)

    return lax.fori_loop(
        1, lax.axis_size(axis), lambda source, state: combine(state, take(source)), take(0)
    )


def partial_softmax(query_tile, key_rows, value_rows, visible):
    score_scale = 1.0 / math.sqrt(key_rows.shape[1])
    scores = (
        jnp.einsum("thd,kd->htk", query_tile, key_rows, preferred_element_type=jnp.float32)
        * score_scale
    )
    scores = jnp.where(visible[None], scores, masked_score)
    row_max = jnp.max(scores, axis=-1)
    weights = jnp.where(visible[None], jnp.exp(scores - row_max[..., None]), 0.0)
    row_total = jnp.sum(weights, axis=-1)
    numerator = jnp.einsum(
        "htk,kd->thd", weights.astype(jnp.bfloat16), value_rows, preferred_element_type=jnp.float32
    )
    return (jnp.transpose(row_max), jnp.transpose(row_total), numerator)


def combine_partials(left_part, right_part):
    max_left, total_left, numer_left = left_part
    max_right, total_right, numer_right = right_part
    row_max = jnp.maximum(max_left, max_right)
    scale_left = jnp.exp(max_left - row_max)
    scale_right = jnp.exp(max_right - row_max)
    return (
        row_max,
        total_left * scale_left + total_right * scale_right,
        numer_left * scale_left[..., None] + numer_right * scale_right[..., None],
    )


def per_device(queries, key_value, block_lists):
    column_count = lax.axis_size("kcol")
    column = lax.axis_index("kcol")
    row_count = lax.axis_size("qrow")
    row_index = lax.axis_index("qrow")
    tok_dev = queries.shape[0]
    feature_count = queries.shape[1]
    head_dim = key_value.shape[1] // 2
    head_count = feature_count // head_dim
    stored = key_value.shape[0] // BLK
    all_blocks = stored * column_count
    gathered = lax.all_gather(queries, "kcol", axis=0, tiled=True)
    gathered_rows = gathered.shape[0]
    tile_rows = BLK // row_count
    query_blocks = gathered_rows // tile_rows
    offset = (all_blocks - query_blocks) * BLK
    gather_pos = jnp.arange(gathered_rows, dtype=jnp.int32)
    token_index = (gather_pos // tok_dev * row_count + row_index) * tok_dev + gather_pos % tok_dev
    query_pos = (offset + token_index).reshape(query_blocks, tile_rows)
    query_tiles = gathered.reshape(query_blocks, tile_rows, head_count, head_dim)
    block_ids = column * stored + jnp.arange(stored, dtype=jnp.int32)
    key_pos = column * stored * BLK + jnp.arange(stored * BLK, dtype=jnp.int32)
    key_rows = key_value[:, :head_dim]
    value_rows = key_value[:, head_dim:]

    def one_block(inputs):
        query_tile, positions, listed = inputs
        listed_here = jnp.any(listed[:, None] == block_ids[None, :], axis=0)
        usable = jnp.repeat(listed_here, BLK, total_repeat_length=stored * BLK)
        visible = usable[None, :] & (key_pos[None, :] <= positions[:, None])
        return partial_softmax(query_tile, key_rows, value_rows, visible)

    row_max, row_total, numerator = lax.map(one_block, (query_tiles, query_pos, block_lists))
    row_max = row_max.reshape(gathered_rows, head_count)
    row_total = row_total.reshape(gathered_rows, head_count)
    numerator = numerator.reshape(gathered_rows, head_count, head_dim)
    merged = combined_all((row_max, row_total, numerator), "kcol", combine_partials)
    first_row = column * tok_dev
    summed_total = lax.dynamic_slice_in_dim(merged[1], first_row, tok_dev, 0)
    summed_numer = lax.dynamic_slice_in_dim(merged[2], first_row, tok_dev, 0)
    attended = summed_numer / summed_total[..., None]
    return attended.reshape(tok_dev, feature_count).astype(jnp.bfloat16)


def solution(mesh):
    placed = (P(("groups", "kcol", "qrow"), None), P(("groups", "kcol"), None), P("groups", None))
    return jax.shard_map(
        per_device,
        mesh=mesh,
        in_specs=placed,
        out_specs=P(("groups", "kcol", "qrow"), None),
        check_vma=False,
    )
```

profile of v0, /device:TPU:0, one launch (start us, length us, event | category | flops | bytes accessed | tf_op | source)
XLA Modules:
  0.0 169.5 jit_solution(10916630586948243898)
XLA Ops:
  8.1 43.3 %all-gather.3 = bf16[16,4,1024]{2,1,0:T(4,128)(2,1)S(1)} all-gather(bf16[1,4,1024]{2,1,0:T(4,128)(2,1)} %bitcast.104), channel_id=1, replica_groups=mesh['groups'=1,'kcol'=16,'qrow'=2] {'kcol'}, dimensions={0}, use_global_device_ids=true | all-gather | bytes 139264 | tf_op jit(solution)/shard_map/all_gather | solution.py:62
  51.5 4.5 %select_reduce_fusion = (pred[1536]{0:T(1024)(128)(4,1)S(1)}, pred[1536]{0:T(1024)(128)(4,1)S(1)}, pred[1536]{0:T(1024)(128)(4,1)S(1)}, pred[1536]{0:T(1024)(128...) fusion(pred[]{:T(512)} %bitcast.11, pred[]{:T(512)} %bitcast.12, pred[]{:T(512)} %bitcast.13, ...), kind=kLoop, calls=%fused_computation.28 | loop fusion | flops 29184 | bytes 21511 | tf_op jit(solution)/shard_map/while/body/eval_jaxpr/jit(_take)/gather | solution.py:79
  56.0 3.2 %fusion.29 = pred[1536]{0:T(1024)(128)(4,1)S(1)} fusion(pred[1536]{0:T(1024)(128)(4,1)S(1)} %get-tuple-element.267, pred[1536]{0:T(1024)(128)(4,1)S(1)} %get-tuple-element.266, pred[1536]{0:T(1024)(128)(4,1)S(1)} %get-tuple-element.265, pred[1536]{0:T(1024)(128)(4,1)S(1)} %get-tuple-element.263, pred[1536]{0:T(1024)(128)(4,1)S(1)} %get-tuple-element.264, ...), kind=kLoop, calls=%fused_computation.47 | loop fusion | flops 21504 | bytes 10757 | tf_op jit(solution)/shard_map/while/body/eval_jaxpr/jit(_take)/select_n | solution.py:79
  59.4 1.7 %fusion.38 = (f32[8,64]{1,0:T(8,128)S(1)}, f32[8,64,1536]{2,1,0:T(8,128)S(1)}) fusion(bf16[64,8,128]{2,1,0:T(8,128)(2,1)S(1)} %squeeze.51, bf16[1536,256]{1,0:T(8,128)(2,1)} %param.8, pred[64,1536]{1,0:T(8,128)(4,1)S(1)} %compare_and_fusion), kind=kOutput, calls=%fused_computation.65 | convolution fusion | flops 203685376 | bytes 3770368 | tf_op jit(solution)/shard_map/while/body/eval_jaxpr/thd,kd->htk/dot_general | solution.py:25
  61.1 1.3 fusion.13
  63.2 36.2 %all-gather.5 = f32[16,64,8]{1,2,0:T(8,128)S(1)} all-gather(f32[1,64,8]{1,2,0:T(8,128)S(1)} %bitcast.103), channel_id=3, replica_groups=mesh['groups'=1,'kcol'=16,'qrow'=2] {'kcol'}, dimensions={0}, use_global_device_ids=true | all-gather | bytes 34816 | tf_op jit(solution)/shard_map/all_gather | solution.py:12
  99.4 39.0 %all-gather.4 = f32[16,64,8]{1,2,0:T(8,128)S(1)} all-gather(f32[1,64,8]{1,2,0:T(8,128)S(1)} %bitcast.102), channel_id=2, replica_groups=mesh['groups'=1,'kcol'=16,'qrow'=2] {'kcol'}, dimensions={0}, use_global_device_ids=true | all-gather | bytes 34816 | tf_op jit(solution)/shard_map/all_gather | solution.py:12
  138.4 1.0 slice.53
  139.6 22.3 %while.26 = (s32[]{:T(128)}, f32[64,8]{0,1:T(8,128)S(1)}, f32[64,8]{0,1:T(8,128)S(1)}, f32[64,8,128]{2,1,0:T(8,128)S(1)}, f32[16,64,8]{1,2,0:T(8,128)S(1)}, /*in...) while((s32[]{:T(128)}, f32[64,8]{0,1:T(8,128)S(1)}, ...), condition=%wide.region_4.5_spmd, body=%wide.region_3.4_spmd.sunk | while | flops 199685 | bytes 1339535 | solution.py:17
  139.8 1.0 constant_dynamic-slice_fusion.3
  141.3 1.0 constant_dynamic-slice_fusion.3
  142.7 1.0 constant_dynamic-slice_fusion.3
  144.2 1.0 constant_dynamic-slice_fusion.3
  145.7 1.0 constant_dynamic-slice_fusion.3
  147.2 1.0 constant_dynamic-slice_fusion.3
  148.7 1.0 constant_dynamic-slice_fusion.3
  150.2 1.0 constant_dynamic-slice_fusion.3
  151.7 1.0 constant_dynamic-slice_fusion.3
  153.1 1.0 constant_dynamic-slice_fusion.3
  154.6 1.0 constant_dynamic-slice_fusion.3
  156.1 1.0 constant_dynamic-slice_fusion.3
  157.6 1.0 constant_dynamic-slice_fusion.3
  159.1 1.0 constant_dynamic-slice_fusion.3
  160.6 1.0 constant_dynamic-slice_fusion.3
  (81 shorter events, 10.8 us)
Async XLA Ops:
  6.5 131.9 %all-gather.8.cloned.1.call-start = ((), (), s32[]{:S(2)}) async-start(), calls=%async_computation | async-start | bytes 4456448 | tf_op jit(solution)/shard_map/all_gather | solution.py:12
  51.5 9.6 %copy-start = (bf16[1536,256]{1,0:T(8,128)(2,1)S(1)}, bf16[1536,256]{1,0:T(8,128)(2,1)}, u32[]{:S(2)}) copy-start(bf16[1536,256]{1,0:T(8,128)(2,1)} %param.8) | copy-start | bytes 2359300
Sparse Core Ops, SparseCore 0:
  62.6 72.8 all-gather.7
where the time goes:
time: 170 us
  blocking collectives  119 us (70%)
  local copies, waits for them, and re-layouts  19.7 us (12%)
  other arithmetic  14.2 us (8%)
  between operations  13.5 us (8%)
  matrix products  3.06 us (2%)
    all_gather x2, blocking collectives, combined_all(): gathered = jax.tree.map(lambda a: lax.all_gather(a, axis), part)  75.2 us
    all_gather x1, blocking collectives, per_device(): gathered = lax.all_gather(queries, 'kcol', axis=0, tiled=True)  43.3 us
    dynamic_slice x18, local copies, waits for them, and re-layouts, take(): lax.dynamic_index_in_dim(a, source, 0, False)  15.5 us
    gather x1, other arithmetic, one_block(): usable = jnp.repeat(listed_here, BLK, total_repeat_length=stored * BLK)  4.49 us
    add x15, other arithmetic, combine_partials(): numer_left * scale_left[..., None] + numer_right * scale_right[..., None]  4.46 us
  transfers between devices with their start and end apart: 1, of which 0 were waited for; matrix products, arithmetic and copies ran while one was open for 0% of the time, Pallas kernels for 0%

commit v1 on v0

--- a/solution.py
+++ b/solution.py
@@ -1,3 +1,4 @@
+import functools
 import math
 import jax
 import jax.numpy as jnp
@@ -6,6 +7,29 @@
 
 BLK = 128
 masked_score = -1e30
+
+
+def _meet_page(piece_in, peer_axis, array_axis):
+    fan = jax.lax.axis_size(peer_axis)
+    so_far_all = [(dev_i, (dev_i + 1) % fan) for dev_i in range(fan)]
+    nodes = [(dev_i, (dev_i - 1) % fan) for dev_i in range(fan)]
+    before, k_now = ([piece_in], [piece_in])
+    for _ in range(fan // 2):
+        before.append(jax.lax.ppermute(before[-1], peer_axis, so_far_all))
+    nth = 0
+    while nth < (fan - 1) // 2:
+        x_new = jax.lax.ppermute(k_now[-1], peer_axis, nodes)
+        k_now.append(x_new)
+        nth = nth + 1
+    high = jnp.concatenate([*before[::-1], *k_now[1:]], axis=array_axis)
+    return jnp.roll(
+        high,
+        (jax.lax.axis_index(peer_axis) - fan // 2) * piece_in.shape[array_axis],
+        axis=array_axis,
+    )
+
+
+fill_the_forms = functools.partial(_meet_page, peer_axis="kcol", array_axis=0)
 
 
 def combined_all(part, axis, combine):
@@ -59,7 +83,7 @@
     head_count = feature_count // head_dim
     stored = key_value.shape[0] // BLK
     all_blocks = stored * column_count
-    gathered = lax.all_gather(queries, "kcol", axis=0, tiled=True)
+    gathered = fill_the_forms(queries)
     gathered_rows = gathered.shape[0]
     tile_rows = BLK // row_count
     query_blocks = gathered_rows // tile_rows

time: 170 us -> 183 us (1.076)
  blocking collectives: 119 us -> 75.3 us
  starting transfers between devices: 0.01 us -> 41.6 us
  other arithmetic: 14.2 us -> 28 us
  waiting for transfers between devices: 0.02 us -> 13 us
  local copies, waits for them, and re-layouts: 19.7 us -> 7.07 us
    all_gather x1 -> x0, blocking collectives: 43.3 us -> none  [per_device(): gathered = lax.all_gather(queries, 'kcol', axis=0, tiled=True)]
    ppermute x0 -> x15, starting transfers between devices: none -> 41.6 us  [the longest x7 38.6 us: _meet_page(): x_new = jax.lax.ppermute(k_now[-1], peer_axis, nodes)]
    dynamic_slice x18 -> x3, local copies, waits for them, and re-layouts: 15.5 us -> 0.97 us  [take(): lax.dynamic_index_in_dim(a, source, 0, False)]
    add x15, other arithmetic: 4.46 us -> 18.1 us  [combine_partials(): numer_left * scale_left[..., None] + numer_right * scale_right[..., None]]
    ppermute x0 -> x15, waiting for transfers between devices: none -> 13 us  [the longest x8 8.62 us: _meet_page(): before.append(jax.lax.ppermute(before[-1], peer_axis, so_far_all))]
    concatenate x0 -> x1, local copies, waits for them, and re-layouts: none -> 1.91 us  [_meet_page(): jnp.roll(high, (jax.lax.axis_index(peer_axis) - fan // 2) * piece_in.shap...]
  transfers between devices with their start and end apart: 1 -> 16, of which waited for: 0 -> 8; matrix products, arithmetic and copies ran while one was open for 0% -> 6% of each run, Pallas kernels for 0% -> 0%
where the time goes in v1:
time: 183 us; the launch traced here: 182 us
  blocking collectives  75.3 us (41%)
  starting transfers between devices  41.6 us (23%)
  other arithmetic  28 us (15%)
  between operations  13.5 us (7%)
  waiting for transfers between devices  13 us (7%)
  local copies, waits for them, and re-layouts  7.07 us (4%)
  matrix products  3.45 us (2%)
    all_gather x2, blocking collectives, combined_all(): gathered = jax.tree.map(lambda a: lax.all_gather(a, axis), part)  75.3 us
    ppermute x7, starting transfers between devices, _meet_page(): x_new = jax.lax.ppermute(k_now[-1], peer_axis, nodes)  38.6 us
    add x15, other arithmetic, combine_partials(): numer_left * scale_left[..., None] + numer_right * scale_right[..., None]  18.1 us
    ppermute x8, waiting for transfers between devices, _meet_page(): before.append(jax.lax.ppermute(before[-1], peer_axis, so_far_all))  8.62 us
    gather x1, other arithmetic, one_block(): usable = jnp.repeat(listed_here, BLK, total_repeat_length=stored * BLK)  4.42 us
    ppermute x7, waiting for transfers between devices, _meet_page(): x_new = jax.lax.ppermute(k_now[-1], peer_axis, nodes)  4.4 us
  transfers between devices with their start and end apart: 16, of which 8 were waited for; matrix products, arithmetic and copies ran while one was open for 6% of the time, Pallas kernels for 0%

profile of v1, /device:TPU:0, one launch (start us, length us, event | category | flops | bytes accessed | tf_op | source)
XLA Modules:
  0.0 182.4 jit_solution(17181877227678484303)
XLA Ops:
  6.5 3.0 %collective-permute-start = (bf16[4,1024]{1,0:T(4,128)(2,1)}, bf16[4,1024]{1,0:T(4,128)(2,1)S(1)}, u32[]{:S(2)}, u32[]{:S(2)}) collective-permute-start(bf16[4,1024]{1,0:T(4,128)(2,1)} %param.7), channel_id=1, source_target_pairs={{0,2},{2,4},{4,6},{6,8},{8,10},{10,12},{12,14},{14,16},{16,18},{18... | collective-permute-start | bytes 24584 | tf_op jit(solution)/shard_map/ppermute | solution.py:18
  9.5 4.0 %collective-permute-start.8 = (bf16[4,1024]{1,0:T(4,128)(2,1)}, bf16[4,1024]{1,0:T(4,128)(2,1)S(1)}, u32[]{:S(2)}, u32[]{:S(2)}) collective-permute-start(bf16[4,1024]{1,0:T(4,128)(2,1)} %param.7), channel_id=1, source_target_pairs={{0,30},{2,0},{4,2},{6,4},{8,6},{10,8},{12,10},{14,12},{16,14},{18,... | collective-permute-start | bytes 24584 | tf_op jit(solution)/shard_map/ppermute | solution.py:21
  16.0 5.7 %collective-permute-start.9 = (bf16[4,1024]{1,0:T(4,128)(2,1)S(1)}, bf16[4,1024]{1,0:T(4,128)(2,1)S(1)}, u32[]{:S(2)}, u32[]{:S(2)}) collective-permute-start(bf16[4,1024]{1,0:T(4,128)(2,1)S(1)} %collective-permute-done.8), channel_id=1, source_target_pairs={{0,30},{2,0},{4,2},{6,4},{8,6},{10,8},{12,10},{14,12},{16,14},{18,... | collective-permute-start | bytes 24584 | tf_op jit(solution)/shard_map/ppermute | solution.py:21
  23.1 5.9 %collective-permute-start.10 = (bf16[4,1024]{1,0:T(4,128)(2,1)S(1)}, bf16[4,1024]{1,0:T(4,128)(2,1)S(1)}, u32[]{:S(2)}, u32[]{:S(2)}) collective-permute-start(bf16[4,1024]{1,0:T(4,128)(2,1)S(1)} %collective-permute-done.9), channel_id=1, source_target_pairs={{0,30},{2,0},{4,2},{6,4},{8,6},{10,8},{12,10},{14,12},{16,14},{18,... | collective-permute-start | bytes 24584 | tf_op jit(solution)/shard_map/ppermute | solution.py:21
  29.8 4.4 %select_reduce_fusion = (pred[1536]{0:T(1024)(128)(4,1)S(1)}, pred[1536]{0:T(1024)(128)(4,1)S(1)}, pred[1536]{0:T(1024)(128)(4,1)S(1)}, pred[1536]{0:T(1024)(128...) fusion(pred[]{:T(512)} %bitcast.11, pred[]{:T(512)} %bitcast.12, pred[]{:T(512)} %bitcast.13, ...), kind=kLoop, calls=%fused_computation.26 | loop fusion | flops 29184 | bytes 21511 | tf_op jit(solution)/shard_map/while/body/eval_jaxpr/jit(_take)/gather | solution.py:103
  34.3 5.7 %collective-permute-start.11 = (bf16[4,1024]{1,0:T(4,128)(2,1)S(1)}, bf16[4,1024]{1,0:T(4,128)(2,1)S(1)}, u32[]{:S(2)}, u32[]{:S(2)}) collective-permute-start(bf16[4,1024]{1,0:T(4,128)(2,1)S(1)} %collective-permute-done.10), channel_id=1, source_target_pairs={{0,30},{2,0},{4,2},{6,4},{8,6},{10,8},{12,10},{14,12},{16,14},{18,... | collective-permute-start | bytes 24584 | tf_op jit(solution)/shard_map/ppermute | solution.py:21
  39.9 3.2 %fusion.27 = pred[1536]{0:T(1024)(128)(4,1)S(1)} fusion(pred[1536]{0:T(1024)(128)(4,1)S(1)} %get-tuple-element.253, pred[1536]{0:T(1024)(128)(4,1)S(1)} %get-tuple-element.252, pred[1536]{0:T(1024)(128)(4,1)S(1)} %get-tuple-element.251, pred[1536]{0:T(1024)(128)(4,1)S(1)} %get-tuple-element.249, pred[1536]{0:T(1024)(128)(4,1)S(1)} %get-tuple-element.250, ...), kind=kLoop, calls=%fused_computation.45 | loop fusion | flops 21504 | bytes 10757 | tf_op jit(solution)/shard_map/while/body/eval_jaxpr/jit(_take)/select_n | solution.py:103
  43.2 5.7 %collective-permute-start.12 = (bf16[4,1024]{1,0:T(4,128)(2,1)S(1)}, bf16[4,1024]{1,0:T(4,128)(2,1)S(1)}, u32[]{:S(2)}, u32[]{:S(2)}) collective-permute-start(bf16[4,1024]{1,0:T(4,128)(2,1)S(1)} %collective-permute-done.11), channel_id=1, source_target_pairs={{0,30},{2,0},{4,2},{6,4},{8,6},{10,8},{12,10},{14,12},{16,14},{18,... | collective-permute-start | bytes 24584 | tf_op jit(solution)/shard_map/ppermute | solution.py:21
  48.9 1.4 collective-permute-done.12
  50.2 5.9 %collective-permute-start.13 = (bf16[4,1024]{1,0:T(4,128)(2,1)S(1)}, bf16[4,1024]{1,0:T(4,128)(2,1)S(1)}, u32[]{:S(2)}, u32[]{:S(2)}) collective-permute-start(bf16[4,1024]{1,0:T(4,128)(2,1)S(1)} %collective-permute-done.12), channel_id=1, source_target_pairs={{0,30},{2,0},{4,2},{6,4},{8,6},{10,8},{12,10},{14,12},{16,14},{18,... | collective-permute-start | bytes 24584 | tf_op jit(solution)/shard_map/ppermute | solution.py:21
  56.1 1.4 collective-permute-done.13
  57.5 5.9 %collective-permute-start.14 = (bf16[4,1024]{1,0:T(4,128)(2,1)S(1)}, bf16[4,1024]{1,0:T(4,128)(2,1)S(1)}, u32[]{:S(2)}, u32[]{:S(2)}) collective-permute-start(bf16[4,1024]{1,0:T(4,128)(2,1)S(1)} %collective-permute-done.13), channel_id=1, source_target_pairs={{0,30},{2,0},{4,2},{6,4},{8,6},{10,8},{12,10},{14,12},{16,14},{18,... | collective-permute-start | bytes 24584 | tf_op jit(solution)/shard_map/ppermute | solution.py:21
  64.7 5.9 %collective-permute-done.7 = bf16[4,1024]{1,0:T(4,128)(2,1)S(1)} collective-permute-done((bf16[4,1024]{1,0:T(4,128)(2,1)S(1)}, bf16[4,1024]{1,0:T(4,128)(2,1)S(1)}, u32[]{:S(2)}, u32[]{:S(2)}) %collective-permute-start.7) | collective-permute-done | bytes 8224 | tf_op jit(solution)/shard_map/ppermute | solution.py:18
  70.6 1.9 %concatenate.12 = bf16[128,1024]{1,0:T(8,128)(2,1)S(1)} concatenate(bf16[4,1024]{1,0:T(4,128)(2,1)S(1)} %collective-permute-done.7, bf16[4,1024]{1,0:T(4,128)(2,1)S(1)} %collective-permute-done.6, bf16[4,1024]{1,0:T(4,128)(2,1)S(1)} %collective-permute-done.5, bf16[4,1024]{1,0:T(4,128)(2,1)S(1)} %collective-permute-done.4, bf16[4,1024]{1,0:T(4,128)(2,1)S(1)} %collective-permute-done.3, ...), dimensions={0} | concatenate | bytes 524288 | tf_op jit(solution)/shard_map/jit(_roll_dynamic)/concatenate | solution.py:25
  72.6 2.0 %fusion.36 = (f32[8,64]{0,1:T(8,128)S(1)}, f32[8,64,1536]{2,0,1:T(8,128)S(1)}) fusion(bf16[64,8,128]{2,1,0:T(8,128)(2,1)S(1)} %bitcast.101, bf16[1536,256]{1,0:T(8,128)(2,1)} %param.8, pred[64,1536]{1,0:T(8,128)(4,1)S(1)} %compare_and_fusion), kind=kOutput, calls=%fused_computation.63 | convolution fusion | flops 203685376 | bytes 3770368 | tf_op jit(solution)/shard_map/while/body/eval_jaxpr/thd,kd->htk/dot_general | solution.py:49
  74.6 1.5 fusion.12
  77.1 36.2 %all-gather.4 = f32[16,64,8]{1,2,0:T(8,128)S(1)} all-gather(f32[1,64,8]{1,2,0:T(8,128)S(1)} %copy.27), channel_id=3, replica_groups=mesh['groups'=1,'kcol'=16,'qrow'=2] {'kcol'}, dimensions={0}, use_global_device_ids=true | all-gather | bytes 34816 | tf_op jit(solution)/shard_map/all_gather | solution.py:36
  113.3 39.1 %all-gather.3 = f32[16,64,8]{1,2,0:T(8,128)S(1)} all-gather(f32[1,64,8]{1,2,0:T(8,128)S(1)} %copy.26), channel_id=2, replica_groups=mesh['groups'=1,'kcol'=16,'qrow'=2] {'kcol'}, dimensions={0}, use_global_device_ids=true | all-gather | bytes 34816 | tf_op jit(solution)/shard_map/all_gather | solution.py:36
  153.4 21.3 %while.26 = (s32[]{:T(128)}, f32[64,8]{0,1:T(8,128)S(1)}, f32[64,8]{0,1:T(8,128)S(1)}, f32[64,8,128]{2,1,0:T(8,128)S(1)}, f32[16,64,8]{1,2,0:T(8,128)S(1)}, /*in...) while((s32[]{:T(128)}, f32[64,8]{0,1:T(8,128)S(1)}, ...), condition=%wide.region_4.5_spmd, body=%wide.region_3.4_spmd.sunk | while | flops 199685 | bytes 815247 | solution.py:41
  153.6 1.2 fusion.41
  155.0 1.2 fusion.41
  156.4 1.2 fusion.41
  157.8 1.2 fusion.41
  159.3 1.2 fusion.41
  (98 shorter events, 23.9 us)
Async XLA Ops:
  6.5 145.9 %all-gather.7.cloned.1.call-start = ((), (), s32[]{:S(2)}) async-start(), calls=%async_computation | async-start | bytes 4456448 | tf_op jit(solution)/shard_map/all_gather | solution.py:36
  6.5 8.8 %collective-permute-start = (bf16[4,1024]{1,0:T(4,128)(2,1)}, bf16[4,1024]{1,0:T(4,128)(2,1)S(1)}, u32[]{:S(2)}, u32[]{:S(2)}) collective-permute-start(bf16[4,1024]{1,0:T(4,128)(2,1)} %param.7), channel_id=1, source_target_pairs={{0,2},{2,4},{4,6},{6,8},{8,10},{10,12},{12,14},{14,16},{16,18},{18... | collective-permute-start | bytes 24584 | tf_op jit(solution)/shard_map/ppermute | solution.py:18
  9.5 6.5 %collective-permute-start.8 = (bf16[4,1024]{1,0:T(4,128)(2,1)}, bf16[4,1024]{1,0:T(4,128)(2,1)S(1)}, u32[]{:S(2)}, u32[]{:S(2)}) collective-permute-start(bf16[4,1024]{1,0:T(4,128)(2,1)} %param.7), channel_id=1, source_target_pairs={{0,30},{2,0},{4,2},{6,4},{8,6},{10,8},{12,10},{14,12},{16,14},{18,... | collective-permute-start | bytes 24584 | tf_op jit(solution)/shard_map/ppermute | solution.py:21
  15.3 7.2 %collective-permute-start.1 = (bf16[4,1024]{1,0:T(4,128)(2,1)S(1)}, bf16[4,1024]{1,0:T(4,128)(2,1)S(1)}, u32[]{:S(2)}, u32[]{:S(2)}) collective-permute-start(bf16[4,1024]{1,0:T(4,128)(2,1)S(1)} %collective-permute-done), channel_id=1, source_target_pairs={{0,2},{2,4},{4,6},{6,8},{8,10},{10,12},{12,14},{14,16},{16,18},{18... | collective-permute-start | bytes 24584 | tf_op jit(solution)/shard_map/ppermute | solution.py:18
  16.0 7.0 %collective-permute-start.9 = (bf16[4,1024]{1,0:T(4,128)(2,1)S(1)}, bf16[4,1024]{1,0:T(4,128)(2,1)S(1)}, u32[]{:S(2)}, u32[]{:S(2)}) collective-permute-start(bf16[4,1024]{1,0:T(4,128)(2,1)S(1)} %collective-permute-done.8), channel_id=1, source_target_pairs={{0,30},{2,0},{4,2},{6,4},{8,6},{10,8},{12,10},{14,12},{16,14},{18,... | collective-permute-start | bytes 24584 | tf_op jit(solution)/shard_map/ppermute | solution.py:21
  22.6 7.2 %collective-permute-start.2 = (bf16[4,1024]{1,0:T(4,128)(2,1)S(1)}, bf16[4,1024]{1,0:T(4,128)(2,1)S(1)}, u32[]{:S(2)}, u32[]{:S(2)}) collective-permute-start(bf16[4,1024]{1,0:T(4,128)(2,1)S(1)} %collective-permute-done.1), channel_id=1, source_target_pairs={{0,2},{2,4},{4,6},{6,8},{8,10},{10,12},{12,14},{14,16},{16,18},{18... | collective-permute-start | bytes 24584 | tf_op jit(solution)/shard_map/ppermute | solution.py:18
  23.1 11.2 %collective-permute-start.10 = (bf16[4,1024]{1,0:T(4,128)(2,1)S(1)}, bf16[4,1024]{1,0:T(4,128)(2,1)S(1)}, u32[]{:S(2)}, u32[]{:S(2)}) collective-permute-start(bf16[4,1024]{1,0:T(4,128)(2,1)S(1)} %collective-permute-done.9), channel_id=1, source_target_pairs={{0,30},{2,0},{4,2},{6,4},{8,6},{10,8},{12,10},{14,12},{16,14},{18,... | collective-permute-start | bytes 24584 | tf_op jit(solution)/shard_map/ppermute | solution.py:21
  29.8 10.1 %collective-permute-start.3 = (bf16[4,1024]{1,0:T(4,128)(2,1)S(1)}, bf16[4,1024]{1,0:T(4,128)(2,1)S(1)}, u32[]{:S(2)}, u32[]{:S(2)}) collective-permute-start(bf16[4,1024]{1,0:T(4,128)(2,1)S(1)} %collective-permute-done.2), channel_id=1, source_target_pairs={{0,2},{2,4},{4,6},{6,8},{8,10},{10,12},{12,14},{14,16},{16,18},{18... | collective-permute-start | bytes 24584 | tf_op jit(solution)/shard_map/ppermute | solution.py:18
  34.3 8.9 %collective-permute-start.11 = (bf16[4,1024]{1,0:T(4,128)(2,1)S(1)}, bf16[4,1024]{1,0:T(4,128)(2,1)S(1)}, u32[]{:S(2)}, u32[]{:S(2)}) collective-permute-start(bf16[4,1024]{1,0:T(4,128)(2,1)S(1)} %collective-permute-done.10), channel_id=1, source_target_pairs={{0,30},{2,0},{4,2},{6,4},{8,6},{10,8},{12,10},{14,12},{16,14},{18,... | collective-permute-start | bytes 24584 | tf_op jit(solution)/shard_map/ppermute | solution.py:21
  39.9 8.9 %collective-permute-start.4 = (bf16[4,1024]{1,0:T(4,128)(2,1)S(1)}, bf16[4,1024]{1,0:T(4,128)(2,1)S(1)}, u32[]{:S(2)}, u32[]{:S(2)}) collective-permute-start(bf16[4,1024]{1,0:T(4,128)(2,1)S(1)} %collective-permute-done.3), channel_id=1, source_target_pairs={{0,2},{2,4},{4,6},{6,8},{8,10},{10,12},{12,14},{14,16},{16,18},{18... | collective-permute-start | bytes 24584 | tf_op jit(solution)/shard_map/ppermute | solution.py:18
  43.2 7.0 %collective-permute-start.12 = (bf16[4,1024]{1,0:T(4,128)(2,1)S(1)}, bf16[4,1024]{1,0:T(4,128)(2,1)S(1)}, u32[]{:S(2)}, u32[]{:S(2)}) collective-permute-start(bf16[4,1024]{1,0:T(4,128)(2,1)S(1)} %collective-permute-done.11), channel_id=1, source_target_pairs={{0,30},{2,0},{4,2},{6,4},{8,6},{10,8},{12,10},{14,12},{16,14},{18,... | collective-permute-start | bytes 24584 | tf_op jit(solution)/shard_map/ppermute | solution.py:21
  48.9 7.2 %collective-permute-start.5 = (bf16[4,1024]{1,0:T(4,128)(2,1)S(1)}, bf16[4,1024]{1,0:T(4,128)(2,1)S(1)}, u32[]{:S(2)}, u32[]{:S(2)}) collective-permute-start(bf16[4,1024]{1,0:T(4,128)(2,1)S(1)} %collective-permute-done.4), channel_id=1, source_target_pairs={{0,2},{2,4},{4,6},{6,8},{8,10},{10,12},{12,14},{14,16},{16,18},{18... | collective-permute-start | bytes 24584 | tf_op jit(solution)/shard_map/ppermute | solution.py:18
  50.2 7.2 %collective-permute-start.13 = (bf16[4,1024]{1,0:T(4,128)(2,1)S(1)}, bf16[4,1024]{1,0:T(4,128)(2,1)S(1)}, u32[]{:S(2)}, u32[]{:S(2)}) collective-permute-start(bf16[4,1024]{1,0:T(4,128)(2,1)S(1)} %collective-permute-done.12), channel_id=1, source_target_pairs={{0,30},{2,0},{4,2},{6,4},{8,6},{10,8},{12,10},{14,12},{16,14},{18,... | collective-permute-start | bytes 24584 | tf_op jit(solution)/shard_map/ppermute | solution.py:21
  56.1 7.2 %collective-permute-start.6 = (bf16[4,1024]{1,0:T(4,128)(2,1)S(1)}, bf16[4,1024]{1,0:T(4,128)(2,1)S(1)}, u32[]{:S(2)}, u32[]{:S(2)}) collective-permute-start(bf16[4,1024]{1,0:T(4,128)(2,1)S(1)} %collective-permute-done.5), channel_id=1, source_target_pairs={{0,2},{2,4},{4,6},{6,8},{8,10},{10,12},{12,14},{14,16},{16,18},{18... | collective-permute-start | bytes 24584 | tf_op jit(solution)/shard_map/ppermute | solution.py:18
  57.5 7.2 %collective-permute-start.14 = (bf16[4,1024]{1,0:T(4,128)(2,1)S(1)}, bf16[4,1024]{1,0:T(4,128)(2,1)S(1)}, u32[]{:S(2)}, u32[]{:S(2)}) collective-permute-start(bf16[4,1024]{1,0:T(4,128)(2,1)S(1)} %collective-permute-done.13), channel_id=1, source_target_pairs={{0,30},{2,0},{4,2},{6,4},{8,6},{10,8},{12,10},{14,12},{16,14},{18,... | collective-permute-start | bytes 24584 | tf_op jit(solution)/shard_map/ppermute | solution.py:21
  63.3 7.2 %collective-permute-start.7 = (bf16[4,1024]{1,0:T(4,128)(2,1)S(1)}, bf16[4,1024]{1,0:T(4,128)(2,1)S(1)}, u32[]{:S(2)}, u32[]{:S(2)}) collective-permute-start(bf16[4,1024]{1,0:T(4,128)(2,1)S(1)} %collective-permute-done.6), channel_id=1, source_target_pairs={{0,2},{2,4},{4,6},{6,8},{8,10},{10,12},{12,14},{14,16},{16,18},{18... | collective-permute-start | bytes 24584 | tf_op jit(solution)/shard_map/ppermute | solution.py:18
  72.5 2.1 %copy-start = (bf16[1536,256]{1,0:T(8,128)(2,1)S(1)}, bf16[1536,256]{1,0:T(8,128)(2,1)}, u32[]{:S(2)}) copy-start(bf16[1536,256]{1,0:T(8,128)(2,1)} %param.8) | copy-start | bytes 2359300
Sparse Core Ops, SparseCore 0:
  76.2 72.0 all-gather.6
